TPU v7x, 512 devices: a whole 4x8x8 slice. The times are simulated.
512 devices in a mesh: dp: 32 (over z, x_hi, core), seq: 16 (over y, x_lo).
Axes of the slice: x: 4 (x_hi: 2, x_lo: 2; x = x_hi * 2 + x_lo), y: 8, z: 8, core: 2. Of those that a mesh axis runs over, the one named last changes fastest.
Arguments:
- features: bfloat16 [32, 2048, 1920], P('dp', 'seq'), may hold values from -48 to 48
- segment_ids: int32 [32, 2048], P('dp'), may hold values from 0 to 7, never falling along the last dimension, each value on 1 to 512 neighbouring positions
- projections: bfloat16 [3, 1920, 1920], P(None, 'seq'), may hold values from -1 to 1
- cotangent: bfloat16 [32, 2048, 1920], P('dp', 'seq'), may hold values from -6 to 6
Outputs:
- context: bfloat16 [32, 2048, 1920], P('dp', 'seq')
- value_grad: float32 [1920, 1920], P('seq')
Inputs may be any that keep to these rules, and one draw needn't show every extreme that they name: `segment_ids`: segment numbers never fall along a sequence; every utterance number appears, each utterance has 1 to 512 frames, and one has exactly 512.
All inputs are finite; a program needn't handle non-finite values.
Results may differ from a plain program's by a relative error of at most 0.011.
Values may be sent and summed in bfloat16 or wider, within the bound.
A program may use at most 64 MiB of HBM per device.

v0:
```python
import jax
import jax.numpy as jnp
from jax import lax
from jax.sharding import PartitionSpec as P

HEAD = 120


def body(features, segment_ids, projections, cotangent):
    frames_local = features[0]
    labels = segment_ids[0]
    local_width = projections.shape[1]
    head_size = HEAD
    local_heads = local_width // head_size
    model_width = frames_local.shape[1]
    weights = projections.reshape(3 * local_width, model_width)
    upstream = lax.all_to_all(cotangent[0], "seq", split_axis=1, concat_axis=0, tiled=True)
    gathered = lax.all_gather(frames_local, "seq", axis=0, tiled=True)
    projected = jnp.einsum(
        "tf,cf->tc", gathered, weights, preferred_element_type=jnp.float32
    ).astype(jnp.bfloat16)
    total_frames = projected.shape[0]
    queries = projected[:, :local_width].reshape(total_frames, local_heads, head_size)
    key_rows = projected[:, local_width : 2 * local_width].reshape(
        total_frames, local_heads, head_size
    )
    values = projected[:, 2 * local_width :].reshape(total_frames, local_heads, head_size)
    upstream_heads = upstream.reshape(total_frames, local_heads, head_size)
    block_rows = min(512, total_frames)
    block_count = total_frames // block_rows
    score_scale = head_size ** (-0.5)

    def weights_of(block_index):
        offset = block_index * block_rows
        query_block = lax.dynamic_slice_in_dim(queries, offset, block_rows, 0)
        row_labels = lax.dynamic_slice_in_dim(labels, offset, block_rows, 0)
        scores = (
            jnp.einsum("qhe,khe->hqk", query_block, key_rows, preferred_element_type=jnp.float32)
            * score_scale
        )
        same_segment = row_labels[:, None] == labels[None, :]
        scores = jnp.where(same_segment[None], scores, -1e30)
        row_max = jnp.max(scores, axis=2, keepdims=True)
        exponent = jnp.exp(scores - row_max)
        attn_weights = (exponent / jnp.sum(exponent, axis=2, keepdims=True)).astype(jnp.bfloat16)
        return (attn_weights, offset)

    def context_of(attn_weights):
        return jnp.einsum(
            "hqk,khe->qhe", attn_weights, values, preferred_element_type=jnp.float32
        ).astype(jnp.bfloat16)

    def value_term(attn_weights, offset):
        grad_block = lax.dynamic_slice_in_dim(upstream_heads, offset, block_rows, 0)
        return jnp.einsum(
            "hqk,qhe->khe", attn_weights, grad_block, preferred_element_type=jnp.float32
        )

    empty_rows = jnp.zeros((total_frames, local_heads, head_size), jnp.float32)

    def joint_step(running, block_index):
        attn_weights, offset = weights_of(block_index)
        return (running + value_term(attn_weights, offset), context_of(attn_weights))

    value_sum, blocks = lax.scan(joint_step, empty_rows, jnp.arange(block_count))
    context = blocks.reshape(total_frames, local_width)
    returned = lax.all_to_all(context, "seq", split_axis=0, concat_axis=1, tiled=True)
    value_rows = value_sum.reshape(total_frames, local_width).astype(jnp.bfloat16)
    partial_grad = jnp.einsum("tw,td->wd", value_rows, gathered, preferred_element_type=jnp.float32)
    summed = lax.psum(partial_grad, "dp")
    value_grad = summed / lax.axis_size("dp")
    return (returned[None], value_grad)


def solution(mesh):
    in_specs = (P("dp", "seq", None), P("dp", None), P(None, "seq", None), P("dp", "seq", None))
    out_specs = (P("dp", "seq", None), P("seq", None))
    return jax.shard_map(body, mesh=mesh, in_specs=in_specs, out_specs=out_specs, check_vma=False)
```

profile of v0, /device:TPU:1, one launch (start us, length us, event | category | flops | bytes accessed | tf_op | source)
XLA Modules:
  0.0 536.6 jit_solution(14925531246365811088)
XLA Ops:
  7.9 2.0 copy.15
  9.9 8.7 %all-to-all-start = ((bf16[128,16,120]{0,2,1:T(8,128)(2,1)}), bf16[128,16,120]{0,2,1:T(8,128)(2,1)S(1)}, u32[]{:S(2)}, u32[]{:S(2)}) async-start(bf16[128,16,120]{0,2,1:T(8,128)(2,1)} %bitcast), calls=%async_computation | async-start | bytes 983040 | tf_op jit(solution)/shard_map/all_to_all | solution.py:17
  18.6 14.4 %all-to-all-done = bf16[128,16,120]{0,2,1:T(8,128)(2,1)S(1)} async-done(((bf16[128,16,120]{0,2,1:T(8,128)(2,1)}), bf16[128,16,120]{0,2,1:T(8,128)(2,1)S(1)}, u32[]{:S(2)}, u32[]{:S(2)}) %all-to-all-start) | async-done | bytes 491552 | tf_op jit(solution)/shard_map/all_to_all | solution.py:17
  34.1 158.1 %all-gather.3.cloned.1.call-done = bf16[1,2048,1920]{2,1,0:T(8,128)(2,1)} async-done(((bf16[1,128,1920]{2,1,0:T(8,128)(2,1)}), bf16[1,2048,1920]{2,1,0:T(8,128)(2,1)}) %all-gather.3.cloned.1.call-update) | async-done | bytes 7864336 | tf_op jit(solution)/shard_map/all_gather | solution.py:18
  192.2 6.5 %fusion.16 = bf16[2048,360]{0,1:T(8,128)(2,1)S(1)} fusion(bf16[360,1920]{1,0:T(8,128)(2,1)S(1)} %bitcast.84, bf16[1,2048,1920]{2,1,0:T(8,128)(2,1)} %all-gather.3.cloned.1.call-done), kind=kOutput, calls=%fused_computation.21 | convolution fusion | flops 2831892480 | bytes 10721280 | tf_op jit(solution)/shard_map/tf,cf->tc/dot_general | solution.py:19
  199.9 36.9 %while.13 = (s32[]{:T(128)}, f32[2048,1,120]{0,2,1:T(8,128)}, bf16[4,512,1,120]{1,3,2,0:T(8,128)(2,1)}, s32[4]{0:T(128)S(1)}, bf16[2048,1,120]{0,2,1:T(8,128)(2,...) while((s32[]{:T(128)}, f32[2048,1,120]{0,2,1:T(8,128)}, ...), condition=%wide.region_3.4_spmd.clone, body=%wide.region_0.3_spmd.clone.sunk | while | flops 764963840 | bytes 24183536 | solution.py:65
  201.3 2.1 fusion.37
  204.8 2.5 fusion.39
  207.3 1.5 fusion.40
  210.2 2.1 fusion.37
  213.8 2.9 fusion.39
  216.6 1.5 fusion.40
  219.5 2.1 fusion.37
  223.1 2.9 fusion.39
  226.0 1.5 fusion.40
  228.8 2.1 fusion.37
  232.4 2.9 fusion.39
  235.3 1.5 fusion.40
  236.7 1.4 copy.17
  239.2 5.3 all-to-all-start.1
  244.6 5.5 %fusion.12 = f32[120,1920]{1,0:T(8,128)} fusion(bf16[1,2048,1920]{2,1,0:T(8,128)(2,1)} %all-gather.3.cloned.1.call-done, f32[2048,1,120]{0,2,1:T(8,128)S(1)} %copy-done.1), kind=kOutput, calls=%fused_computation.17 | convolution fusion | flops 943964160 | bytes 9768960 | tf_op jit(solution)/shard_map/tw,td->wd/dot_general | solution.py:69
  250.1 9.5 %all-to-all-done.1 = bf16[16,128,120]{1,2,0:T(8,128)(2,1)S(1)} async-done(((bf16[16,128,120]{1,2,0:T(8,128)(2,1)}), bf16[16,128,120]{1,2,0:T(8,128)(2,1)S(1)}, u32[]{:S(2)}, u32[]{:S(2)}) %all-to-all-start.1) | async-done | bytes 491552 | tf_op jit(solution)/shard_map/all_to_all | solution.py:67
  260.6 267.0 %all-reduce.2.cloned.1.call-done = f32[120,1920]{1,0:T(8,128)} async-done(((f32[120,1920]{1,0:T(8,128)}), f32[120,1920]{1,0:T(8,128)}) %all-reduce.2.cloned.1.call-update) | async-done | bytes 921616 | tf_op jit(solution)/shard_map/psum | solution.py:70
  527.6 2.2 broadcast_multiply_fusion
  (43 shorter events, 14.0 us)
Async XLA Ops:
  7.2 185.0 %copy-start = (bf16[3,120,1920]{2,1,0:T(8,128)(2,1)S(1)}, bf16[3,120,1920]{2,1,0:T(8,128)(2,1)}, u32[]{:S(2)}) copy-start(bf16[3,120,1920]{2,1,0:T(8,128)(2,1)} %param.8) | copy-start | bytes 4147204
  7.2 185.0 %all-gather.3.cloned.1.call-start = ((), (), s32[]{:S(2)}) async-start(), calls=%async_computation.3 | async-start | bytes 8355840 | tf_op jit(solution)/shard_map/all_gather | solution.py:18
  9.9 23.1 %all-to-all-start = ((bf16[128,16,120]{0,2,1:T(8,128)(2,1)}), bf16[128,16,120]{0,2,1:T(8,128)(2,1)S(1)}, u32[]{:S(2)}, u32[]{:S(2)}) async-start(bf16[128,16,120]{0,2,1:T(8,128)(2,1)} %bitcast), calls=%async_computation | async-start | bytes 983040 | tf_op jit(solution)/shard_map/all_to_all | solution.py:17
  192.2 7.7 %copy-start.3 = (s32[1,2048]{1,0:T(1,128)S(1)}, s32[1,2048]{1,0:T(1,128)}, u32[]{:S(2)}) copy-start(s32[1,2048]{1,0:T(1,128)} %param.7) | copy-start | bytes 24580
  204.8 2.5 copy-start.2
  213.8 2.9 copy-start.2
  223.1 2.9 copy-start.2
  232.4 2.9 copy-start.2
  236.7 7.9 %copy-start.1 = (f32[2048,1,120]{0,2,1:T(8,128)S(1)}, f32[2048,1,120]{0,2,1:T(8,128)}, u32[]{:S(2)}) copy-start(f32[2048,1,120]{0,2,1:T(8,128)} %get-tuple-element.56) | copy-start | bytes 2949124
  239.2 20.3 %all-to-all-start.1 = ((bf16[16,128,120]{1,2,0:T(8,128)(2,1)}), bf16[16,128,120]{1,2,0:T(8,128)(2,1)S(1)}, u32[]{:S(2)}, u32[]{:S(2)}) async-start(bf16[16,128,120]{1,2,0:T(8,128)(2,1)} %copy.18), calls=%async_computation.1 | async-start | bytes 983040 | tf_op jit(solution)/shard_map/all_to_all | solution.py:67
  244.6 283.0 %all-reduce.2.cloned.1.call-start = ((), (), s32[]{:S(2)}) async-start(), calls=%async_computation.2 | async-start | bytes 1843200 | tf_op jit(solution)/shard_map/psum | solution.py:70
Sparse Core Ops, SparseCore 0:
  10.1 182.0 all-gather.2
  250.2 277.2 all-reduce.1
where the time goes:
time: 537 us
  waiting for transfers between devices  450 us (84%)
  matrix products  37.2 us (7%)
  starting transfers between devices  14.1 us (3%)
  between operations  14.1 us (3%)
  local copies, waits for them, and re-layouts  10.7 us (2%)
  other arithmetic  8.07 us (2%)
    psum x1, waiting for transfers between devices, body(): summed = lax.psum(partial_grad, 'dp')  267 us
    all_gather x1, waiting for transfers between devices, body(): gathered = lax.all_gather(frames_local, 'seq', axis=0, tiled=True)  158 us
    all_to_all x1, waiting for transfers between devices, body(): lax.all_to_all(cotangent[0], 'seq', split_axis=1, concat_axis=0, tiled=True)  14.4 us
    dot_general x4, matrix products, value_term(): jnp.einsum('hqk,qhe->khe', attn_weights, grad_block, preferred_element_ty...  11.1 us
  transfers between devices with their start and end apart: 4, of which 4 were waited for; matrix products, arithmetic and copies ran while one was open for 2% of the time, Pallas kernels for 0%

commit v1 on v0

--- a/solution.py
+++ b/solution.py
@@ -67,7 +67,8 @@
     returned = lax.all_to_all(context, "seq", split_axis=0, concat_axis=1, tiled=True)
     value_rows = value_sum.reshape(total_frames, local_width).astype(jnp.bfloat16)
     partial_grad = jnp.einsum("tw,td->wd", value_rows, gathered, preferred_element_type=jnp.float32)
-    summed = lax.psum(partial_grad, "dp")
+    shards = lax.all_gather(partial_grad, "dp", axis=0, tiled=False)
+    summed = shards.sum(axis=0)
     value_grad = summed / lax.axis_size("dp")
     return (returned[None], value_grad)
 

time: 537 us -> 466 us (0.87)
  waiting for transfers between devices: 450 us -> 366 us
  blocking collectives: 0 us -> 20.1 us
  other arithmetic: 8.07 us -> 18 us
  matrix products: 37.2 us -> 28.6 us
    psum x1 -> x0, waiting for transfers between devices: 267 us -> none  [body(): summed = lax.psum(partial_grad, 'dp')]
    all_gather x0 -> x1, waiting for transfers between devices: none -> 193 us  [body(): shards = lax.all_gather(partial_grad, 'dp', axis=0, tiled=False)]
    all_to_all x0 -> x1, blocking collectives: none -> 20.1 us  [body(): lax.all_to_all(context, 'seq', split_axis=0, concat_axis=1, tiled=True)]
    reduce_sum x0 -> x1, other arithmetic: none -> 11.1 us  [body(): summed = shards.sum(axis=0)]
    all_to_all x1 -> x0, waiting for transfers between devices: 9.45 us -> none  [body(): lax.all_to_all(context, 'seq', split_axis=0, concat_axis=1, tiled=True)]
    dot_general x4, matrix products: 11.1 us -> 2.36 us  [value_term(): jnp.einsum('hqk,qhe->khe', attn_weights, grad_block, preferred_element_ty...]
  transfers between devices with their start and end apart: 4 -> 3, of which waited for: 4 -> 3; matrix products, arithmetic and copies ran while one was open for 2% -> 1% of each run, Pallas kernels for 0% -> 0%
where the time goes in v1:
time: 466 us
  waiting for transfers between devices  366 us (79%)
  matrix products  28.6 us (6%)
  blocking collectives  20.1 us (4%)
  other arithmetic  18 us (4%)
  between operations  14.1 us (3%)
  starting transfers between devices  8.75 us (2%)
  local copies, waits for them, and re-layouts  7.52 us (2%)
    all_gather x1, waiting for transfers between devices, body(): shards = lax.all_gather(partial_grad, 'dp', axis=0, tiled=False)  193 us
    all_gather x1, waiting for transfers between devices, body(): gathered = lax.all_gather(frames_local, 'seq', axis=0, tiled=True)  159 us
    all_to_all x1, blocking collectives, body(): lax.all_to_all(context, 'seq', split_axis=0, concat_axis=1, tiled=True)  20.1 us
    all_to_all x1, waiting for transfers between devices, body(): lax.all_to_all(cotangent[0], 'seq', split_axis=1, concat_axis=0, tiled=True)  14.4 us
    reduce_sum x1, other arithmetic, body(): summed = shards.sum(axis=0)  11.1 us
  transfers between devices with their start and end apart: 3, of which 3 were waited for; matrix products, arithmetic and copies ran while one was open for 1% of the time, Pallas kernels for 0%

profile of v1, /device:TPU:1, one launch (start us, length us, event | category | flops | bytes accessed | tf_op | source)
XLA Modules:
  0.0 465.9 jit_solution(2555591632443291130)
XLA Ops:
  7.9 2.0 copy.15
  9.9 8.7 %all-to-all-start = ((bf16[128,16,120]{0,2,1:T(8,128)(2,1)}), bf16[128,16,120]{0,2,1:T(8,128)(2,1)S(1)}, u32[]{:S(2)}, u32[]{:S(2)}) async-start(bf16[128,16,120]{0,2,1:T(8,128)(2,1)} %bitcast), calls=%async_computation | async-start | bytes 983040 | tf_op jit(solution)/shard_map/all_to_all | solution.py:17
  18.7 14.4 %all-to-all-done = bf16[128,16,120]{0,2,1:T(8,128)(2,1)S(1)} async-done(((bf16[128,16,120]{0,2,1:T(8,128)(2,1)}), bf16[128,16,120]{0,2,1:T(8,128)(2,1)S(1)}, u32[]{:S(2)}, u32[]{:S(2)}) %all-to-all-start) | async-done | bytes 491552 | tf_op jit(solution)/shard_map/all_to_all | solution.py:17
  33.3 158.8 %all-gather.5.cloned.1.call-done = bf16[1,2048,1920]{2,1,0:T(8,128)(2,1)} async-done(((bf16[1,128,1920]{2,1,0:T(8,128)(2,1)}), bf16[1,2048,1920]{2,1,0:T(8,128)(2,1)}) %all-gather.5.cloned.1.call-update) | async-done | bytes 7864336 | tf_op jit(solution)/shard_map/all_gather | solution.py:18
  192.2 6.5 %fusion.16 = bf16[2048,360]{0,1:T(8,128)(2,1)S(1)} fusion(bf16[360,1920]{1,0:T(8,128)(2,1)S(1)} %bitcast.85, bf16[1,2048,1920]{2,1,0:T(8,128)(2,1)} %all-gather.5.cloned.1.call-done), kind=kOutput, calls=%fused_computation.21 | convolution fusion | flops 2831892480 | bytes 10721280 | tf_op jit(solution)/shard_map/tf,cf->tc/dot_general | solution.py:19
  198.7 1.1 slice_bitcast_fusion
  199.8 27.3 %while.13 = (s32[]{:T(128)}, f32[2048,1,120]{0,2,1:T(8,128)S(1)}, bf16[4,512,1,120]{1,3,2,0:T(8,128)(2,1)}, s32[4]{0:T(128)S(1)}, bf16[2048,1,120]{0,2,1:T(8,128...) while((s32[]{:T(128)}, f32[2048,1,120]{0,2,1:T(8,128)S(1)}, ...), condition=%wide.region_3.4_spmd.clone, body=%wide.region_0.3_spmd.clone.sunk | while | flops 764963840 | bytes 22216928 | solution.py:65
  201.0 2.1 fusion.37
  203.7 0.8 divide_convert_fusion.2
  204.5 1.5 fusion.40
  207.8 2.1 fusion.37
  211.4 1.5 fusion.40
  214.6 2.1 fusion.37
  217.4 0.8 divide_convert_fusion.2
  218.2 1.5 fusion.40
  221.5 2.1 fusion.37
  224.2 0.8 divide_convert_fusion.2
  225.0 1.5 fusion.40
  227.1 5.5 %fusion.12 = f32[120,1920]{1,0:T(8,128)} fusion(bf16[1,2048,1920]{2,1,0:T(8,128)(2,1)} %all-gather.5.cloned.1.call-done, f32[2048,1,120]{0,2,1:T(8,128)S(1)} %get-tuple-element.56), kind=kOutput, calls=%fused_computation.17 | convolution fusion | flops 943964160 | bytes 9768960 | tf_op jit(solution)/shard_map/tw,td->wd/dot_general | solution.py:69
  233.3 20.1 %all_to_all.32 = bf16[16,128,120]{1,2,0:T(8,128)(2,1)S(1)} all-to-all(bf16[16,128,120]{1,2,0:T(8,128)(2,1)S(1)} %copy.18), channel_id=1, replica_groups=mesh['dp'=32,'seq'=16] {'seq'}, dimensions={0} | all-to-all | bytes 983040 | tf_op jit(solution)/shard_map/all_to_all | solution.py:67
  253.4 1.0 copy.19
  254.4 192.5 %all-gather.7.cloned.1.call-done = f32[3840,1920]{1,0:T(8,128)} async-done(((f32[120,1920]{1,0:T(8,128)}), f32[3840,1920]{1,0:T(8,128)}) %all-gather.7.cloned.1.call-update) | async-done | bytes 29491216 | tf_op jit(solution)/shard_map/all_gather | solution.py:70
  446.9 11.1 %reduce_sum.18 = f32[120,1920]{1,0:T(8,128)S(1)} reduce(f32[32,120,1920]{2,1,0:T(8,128)} %bitcast.86, f32[]{:T(128)} %constant.23.clone.1), dimensions={0}, to_apply=%region_4.5 | reduce | flops 7142400 | bytes 30412804 | tf_op jit(solution)/shard_map/reduce_sum | solution.py:71
  458.1 1.0 broadcast_multiply_fusion
  (35 shorter events, 10.1 us)
Async XLA Ops:
  7.2 185.0 %copy-start = (bf16[3,120,1920]{2,1,0:T(8,128)(2,1)S(1)}, bf16[3,120,1920]{2,1,0:T(8,128)(2,1)}, u32[]{:S(2)}) copy-start(bf16[3,120,1920]{2,1,0:T(8,128)(2,1)} %param.8) | copy-start | bytes 4147204
  7.2 185.0 %all-gather.5.cloned.1.call-start = ((), (), s32[]{:S(2)}) async-start(), calls=%async_computation.2 | async-start | bytes 8355840 | tf_op jit(solution)/shard_map/all_gather | solution.py:18
  9.9 23.1 %all-to-all-start = ((bf16[128,16,120]{0,2,1:T(8,128)(2,1)}), bf16[128,16,120]{0,2,1:T(8,128)(2,1)S(1)}, u32[]{:S(2)}, u32[]{:S(2)}) async-start(bf16[128,16,120]{0,2,1:T(8,128)(2,1)} %bitcast), calls=%async_computation | async-start | bytes 983040 | tf_op jit(solution)/shard_map/all_to_all | solution.py:17
  18.6 428.3 %all-gather.7.cloned.1.call-start = ((), (), s32[]{:S(2)}) async-start(), calls=%async_computation.3 | async-start | bytes 30412800 | tf_op jit(solution)/shard_map/all_gather | solution.py:70
  192.2 7.6 %copy-start.2 = (s32[1,2048]{1,0:T(1,128)S(1)}, s32[1,2048]{1,0:T(1,128)}, u32[]{:S(2)}) copy-start(s32[1,2048]{1,0:T(1,128)} %param.7) | copy-start | bytes 24580
  227.1 5.6 %copy-start.1 = (bf16[4,512,1,120]{1,3,2,0:T(8,128)(2,1)S(1)}, bf16[4,512,1,120]{1,3,2,0:T(8,128)(2,1)}, u32[]{:S(2)}) copy-start(bf16[4,512,1,120]{1,3,2,0:T(8,128)(2,1)} %get-tuple-element.55) | copy-start | bytes 1474564
Sparse Core Ops, SparseCore 0:
  10.1 182.0 all-gather.4
  232.8 214.1 all-gather.6

commit v2 on v0

--- a/solution.py
+++ b/solution.py
@@ -4,6 +4,13 @@
 from jax.sharding import PartitionSpec as P
 
 HEAD = 120
+
+
+def gather_over(x, axis, d):
+    size = lax.axis_size(axis)
+    blocks = jnp.stack([x for _ in range(size)])
+    blocks = lax.all_to_all(blocks, axis, split_axis=0, concat_axis=0)
+    return jnp.concatenate(blocks, axis=d)
 
 
 def body(features, segment_ids, projections, cotangent):
@@ -15,7 +22,7 @@
     model_width = frames_local.shape[1]
     weights = projections.reshape(3 * local_width, model_width)
     upstream = lax.all_to_all(cotangent[0], "seq", split_axis=1, concat_axis=0, tiled=True)
-    gathered = lax.all_gather(frames_local, "seq", axis=0, tiled=True)
+    gathered = gather_over(frames_local, "seq", 0)
     projected = jnp.einsum(
         "tf,cf->tc", gathered, weights, preferred_element_type=jnp.float32
     ).astype(jnp.bfloat16)

time: 537 us -> 567 us (1.056)
  blocking collectives: 0 us -> 23.5 us
    all_to_all x1, waiting for transfers between devices: 14.4 us -> 178 us  [gather_over(): blocks = lax.all_to_all(blocks, axis, split_axis=0, concat_axis=0)]
    all_gather x1 -> x0, waiting for transfers between devices: 158 us -> none  [body(): gathered = lax.all_gather(frames_local, 'seq', axis=0, tiled=True)]
    all_to_all x0 -> x1, blocking collectives: none -> 23.5 us  [body(): lax.all_to_all(cotangent[0], 'seq', split_axis=1, concat_axis=0, tiled=True)]
  transfers between devices with their start and end apart: 4 -> 3, of which waited for: 4 -> 3; matrix products, arithmetic and copies ran while one was open for 2% -> 1% of each run, Pallas kernels for 0% -> 0%
where the time goes in v2:
time: 567 us; the launch traced here: 566 us
  waiting for transfers between devices  455 us (80%)
  matrix products  36.8 us (6%)
  blocking collectives  23.5 us (4%)
  local copies, waits for them, and re-layouts  15.2 us (3%)
  between operations  14.1 us (2%)
  starting transfers between devices  10.4 us (2%)
  other arithmetic  8.07 us (1%)
    psum x1, waiting for transfers between devices, body(): summed = lax.psum(partial_grad, 'dp')  269 us
    all_to_all x1, waiting for transfers between devices, gather_over(): blocks = lax.all_to_all(blocks, axis, split_axis=0, concat_axis=0)  178 us
    all_to_all x1, blocking collectives, body(): lax.all_to_all(cotangent[0], 'seq', split_axis=1, concat_axis=0, tiled=True)  23.5 us
  transfers between devices with their start and end apart: 3, of which 3 were waited for; matrix products, arithmetic and copies ran while one was open for 1% of the time, Pallas kernels for 0%

profile of v2, /device:TPU:1, one launch (start us, length us, event | category | flops | bytes accessed | tf_op | source)
XLA Modules:
  0.0 566.0 jit_solution(11994227106076140526)
XLA Ops:
  7.2 1.4 copy.15
  8.6 23.5 %all_to_all.37 = bf16[128,16,120]{0,2,1:T(8,128)(2,1)S(1)} all-to-all(bf16[128,16,120]{0,2,1:T(8,128)(2,1)S(1)} %bitcast.84), channel_id=1, replica_groups=mesh['dp'=32,'seq'=16] {'seq'}, dimensions={1} | all-to-all | bytes 983040 | tf_op jit(solution)/shard_map/all_to_all | solution.py:24
  32.1 5.2 stack.3
  37.4 4.7 all-to-all-start.1
  43.2 177.8 %all-to-all-done.1 = bf16[16,128,1920]{2,1,0:T(8,128)(2,1)} async-done(((bf16[16,128,1920]{2,1,0:T(8,128)(2,1)}), bf16[16,128,1920]{2,1,0:T(8,128)(2,1)}, u32[]{:S(2)}, u32[]{:S(2)}) %all-to-all-start.1) | async-done | bytes 7864352 | tf_op jit(solution)/shard_map/all_to_all | solution.py:12
  221.0 6.5 %convolution_convert_fusion.1 = bf16[2048,360]{0,1:T(8,128)(2,1)S(1)} fusion(bf16[2048,1920]{1,0:T(8,128)(2,1)} %bitcast.4, bf16[360,1920]{1,0:T(8,128)(2,1)S(1)} %bitcast.81), kind=kOutput, calls=%fused_computation.17 | convolution fusion | flops 2831892480 | bytes 10721280 | tf_op jit(solution)/shard_map/tf,cf->tc/dot_general | solution.py:26
  228.7 36.3 %while.13 = (s32[]{:T(128)}, f32[2048,1,120]{0,2,1:T(8,128)}, bf16[4,512,1,120]{1,3,2,0:T(8,128)(2,1)}, s32[4]{0:T(128)S(1)}, bf16[2048,1,120]{0,2,1:T(8,128)(2,...) while((s32[]{:T(128)}, f32[2048,1,120]{0,2,1:T(8,128)}, ...), condition=%wide.region_3.4_spmd.clone, body=%wide.region_0.3_spmd.clone.sunk | while | flops 764963840 | bytes 24183536 | solution.py:72
  230.0 2.1 fusion.33
  233.6 2.4 fusion.35
  236.0 1.5 fusion.36
  238.8 2.1 fusion.33
  242.4 2.8 fusion.35
  245.2 1.5 fusion.36
  248.0 2.1 fusion.33
  251.6 2.8 fusion.35
  254.3 1.5 fusion.36
  257.2 2.1 fusion.33
  260.7 2.8 fusion.35
  263.5 1.5 fusion.36
  267.4 5.6 all-to-all-start.2
  273.1 5.5 fusion.12
  278.6 8.8 %all-to-all-done.2 = bf16[16,128,120]{1,2,0:T(8,128)(2,1)S(1)} async-done(((bf16[16,128,120]{1,2,0:T(8,128)(2,1)}), bf16[16,128,120]{1,2,0:T(8,128)(2,1)S(1)}, u32[]{:S(2)}, u32[]{:S(2)}) %all-to-all-start.2) | async-done | bytes 491552 | tf_op jit(solution)/shard_map/all_to_all | solution.py:74
  288.4 268.6 %all-reduce.2.cloned.1.call-done = f32[120,1920]{1,0:T(8,128)} async-done(((f32[120,1920]{1,0:T(8,128)}), f32[120,1920]{1,0:T(8,128)}) %all-reduce.2.cloned.1.call-update) | async-done | bytes 921616 | tf_op jit(solution)/shard_map/psum | solution.py:77
  557.0 2.2 broadcast_multiply_fusion
  (42 shorter events, 14.6 us)
Async XLA Ops:
  7.2 213.8 %copy-start = (bf16[3,120,1920]{2,1,0:T(8,128)(2,1)S(1)}, bf16[3,120,1920]{2,1,0:T(8,128)(2,1)}, u32[]{:S(2)}) copy-start(bf16[3,120,1920]{2,1,0:T(8,128)(2,1)} %param.8) | copy-start | bytes 4147204
  37.4 183.6 %all-to-all-start.1 = ((bf16[16,128,1920]{2,1,0:T(8,128)(2,1)}), bf16[16,128,1920]{2,1,0:T(8,128)(2,1)}, u32[]{:S(2)}, u32[]{:S(2)}) async-start(bf16[16,128,1920]{2,1,0:T(8,128)(2,1)} %stack.3), calls=%async_computation.1 | async-start | bytes 15728640 | tf_op jit(solution)/shard_map/all_to_all | solution.py:12
  221.0 7.7 %copy-start.3 = (s32[1,2048]{1,0:T(1,128)S(1)}, s32[1,2048]{1,0:T(1,128)}, u32[]{:S(2)}) copy-start(s32[1,2048]{1,0:T(1,128)} %param.7) | copy-start | bytes 24580
  233.6 2.4 copy-start.2
  242.4 2.8 copy-start.2
  251.6 2.8 copy-start.2
  260.7 2.8 copy-start.2
  265.0 8.2 %copy-start.1 = (f32[2048,1,120]{0,2,1:T(8,128)S(1)}, f32[2048,1,120]{0,2,1:T(8,128)}, u32[]{:S(2)}) copy-start(f32[2048,1,120]{0,2,1:T(8,128)} %get-tuple-element.56) | copy-start | bytes 2949124
  267.4 19.9 %all-to-all-start.2 = ((bf16[16,128,120]{1,2,0:T(8,128)(2,1)}), bf16[16,128,120]{1,2,0:T(8,128)(2,1)S(1)}, u32[]{:S(2)}, u32[]{:S(2)}) async-start(bf16[16,128,120]{1,2,0:T(8,128)(2,1)} %copy.18), calls=%async_computation.2 | async-start | bytes 983040 | tf_op jit(solution)/shard_map/all_to_all | solution.py:74
  273.1 283.9 %all-reduce.2.cloned.1.call-start = ((), (), s32[]{:S(2)}) async-start(), calls=%async_computation.3 | async-start | bytes 1843200 | tf_op jit(solution)/shard_map/psum | solution.py:77
Sparse Core Ops, SparseCore 0:
  278.7 278.2 all-reduce.1
